TPU v7x, 32 devices: a whole 2x2x4 slice. The times are simulated.
32 devices in a mesh: fields: 2 (over y), rows: 4 (over z), cols: 2 (over x), sub: 2 (over core).
Axes of the slice: x: 2, y: 2, z: 4, core: 2. Of those that a mesh axis runs over, the one named last changes fastest.
Arguments:
- convergence: bfloat16 [32, 32, 16, 512], P(('fields', 'rows'), 'cols'), parts along dimension 0, may hold values from -6 to 6
- block_level: int32 [32, 32], P(('fields', 'rows'), 'cols'), parts along dimension 0, may hold values from 0 to 1
- near_codes: int32 [32, 32, 8], P(('fields', 'rows'), 'cols', 'sub'), parts along dimension 0, may hold values from 0 to 24, as said below
- far_rows: int32 [32, 32, 4], P(('fields', 'rows'), 'cols', 'sub'), parts along dimension 0, may hold values from 0 to 15, as said below
- near_factor: bfloat16 [512, 4096], P(None, 'sub'), may hold values from -0.09375 to 0.09375
- far_factor: bfloat16 [512, 2048], P(None, 'sub'), may hold values from -0.125 to 0.125
Outputs:
- whitened: bfloat16 [32, 32, 16, 512], P(('fields', 'rows'), 'cols', 'sub'), parts along dimension 0
There are 2 independent parts, one for each index of `fields`. A program takes and returns all parts, laid end to end along the dimension named above; an argument that names none is the same for every part. Nothing has to cross between parts.
Inputs may be any that keep to these rules, and one draw needn't show every extreme that they name: `near_codes`: the 8 codes of a block are different from one another and never 12 (the block itself). `far_rows`: an entry never names a block row held by the same index of rows as the block. Among the 128 entries that one index of rows, cols and sub holds (slots 0 to 1 or 2 to 3), each other index of rows is named at most 64 times through its block rows, and one is named exactly 64 times.
All inputs are finite; a program needn't handle non-finite values.
Results may differ from a plain program's by a relative error of at most 0.001.
Values may be sent and summed in bfloat16 or wider, within the bound.
A program may use at most 64 MiB of HBM per device.

v0:
```python
import jax
import jax.numpy as jnp
from jax import lax
from jax.sharding import PartitionSpec as P


def padded(array, sides, width):
    for axis, dim in sides:
        count, length = (lax.axis_size(axis), array.shape[dim])
        up = [(i, (i + 1) % count) for i in range(count - 1)]
        down = [(j, i) for i, j in up]
        last = lax.slice_in_dim(array, length - width, length, axis=dim)
        first = lax.slice_in_dim(array, 0, width, axis=dim)
        before = lax.ppermute(last, axis, up)
        after = lax.ppermute(first, axis, down)
        array = jnp.concatenate([before, array, after], axis=dim)
    return array


def on_device(convergence, block_level, near_codes, far_rows, near_factor, far_factor):
    tile_rows, tile_cols, samples, pixels = convergence.shape
    block_count = tile_rows * tile_cols
    sub_index = lax.axis_index("sub")
    half_count = samples // 2
    extended = padded(convergence, (("rows", 0), ("cols", 1)), 2)
    flat_ext = extended.reshape((tile_rows + 4) * (tile_cols + 4), samples, pixels)
    row_pos = jnp.arange(tile_rows, dtype=jnp.int32)[:, None, None]
    col_pos = jnp.arange(tile_cols, dtype=jnp.int32)[None, :, None]
    near_index = (row_pos + near_codes // 5) * (tile_cols + 4) + col_pos + near_codes % 5
    near_slots = near_codes.shape[2]
    near_blocks = jnp.take(flat_ext, near_index.reshape(-1), axis=0).reshape(
        block_count, near_slots, samples, pixels
    )
    near_terms = lax.dot_general(
        near_blocks,
        near_factor.reshape(pixels, near_slots, pixels),
        (((1, 3), (1, 2)), ((), ())),
        preferred_element_type=jnp.float32,
    )
    requests = far_rows.reshape(-1)
    far_slots = far_rows.shape[2]
    flat_tile = convergence.reshape(block_count, samples, pixels)
    request_cols = jnp.arange(requests.shape[0], dtype=jnp.int32) // far_slots % tile_cols
    empty = jnp.zeros((requests.shape[0], samples, pixels), jnp.bfloat16)
    piece = lax.all_gather(convergence, "rows", axis=0, tiled=True)
    start = jnp.int32(0)
    piece_rows = piece.shape[0]
    flat_piece = piece.reshape(piece_rows * tile_cols, samples, pixels)
    inside = (requests >= start) & (requests < start + piece_rows)
    local = jnp.clip(requests * tile_cols + request_cols, 0, piece_rows * tile_cols - 1)
    found = jnp.take(flat_piece, local, axis=0)
    far_flat = jnp.where(inside[:, None, None], found, empty)
    far_blocks = far_flat.reshape(block_count, far_slots, samples, pixels)
    far_terms = lax.dot_general(
        far_blocks,
        far_factor.reshape(pixels, far_slots, pixels),
        (((1, 3), (1, 2)), ((), ())),
        preferred_element_type=jnp.float32,
    )
    level_flat = block_level.reshape(block_count)
    partial_value = jnp.where(level_flat[:, None, None] == 1, near_terms, far_terms)
    mean_half = lax.psum_scatter(partial_value, "sub", scatter_dimension=1, tiled=True)
    own_half = lax.dynamic_slice_in_dim(flat_tile, sub_index * half_count, half_count, 1)
    whitened = (own_half.astype(jnp.float32) - mean_half).astype(jnp.bfloat16)
    return whitened.reshape(tile_rows, tile_cols, half_count, pixels)


def solution(mesh):
    placed = (
        P(("fields", "rows"), "cols", None, None),
        P(("fields", "rows"), "cols"),
        P(("fields", "rows"), "cols", "sub"),
        P(("fields", "rows"), "cols", "sub"),
        P(None, "sub"),
        P(None, "sub"),
    )
    return jax.shard_map(
        on_device,
        mesh=mesh,
        in_specs=placed,
        out_specs=P(("fields", "rows"), "cols", "sub", None),
        check_vma=False,
    )
```

profile of v0, /device:TPU:0, one launch (start us, length us, event | category | flops | bytes accessed | tf_op | source)
XLA Modules:
  0.0 126.5 jit_solution(18052864852191408466)
XLA Ops:
  6.6 0.7 all-gather.2.cloned.1.call-update
  7.3 1.3 %fusion.15 = (bf16[2,16,16,512]{3,2,1,0:T(8,128)(2,1)S(1)}, bf16[2,16,16,512]{3,2,1,0:T(8,128)(2,1)S(1)}) fusion(bf16[4,16,16,512]{3,2,1,0:T(8,128)(2,1)} %param.6), kind=kLoop, calls=%fused_computation.56 | loop fusion | bytes 2097152 | tf_op jit(solution)/shard_map/slice | solution.py:13
  8.6 1.3 %collective-permute-start.1 = (bf16[2,16,16,512]{3,2,1,0:T(8,128)(2,1)S(1)}, bf16[2,16,16,512]{3,2,1,0:T(8,128)(2,1)S(1)}, u32[]{:S(2)}, u32[]{:S(2)}) collective-permute-start(bf16[2,16,16,512]{3,2,1,0:T(8,128)(2,1)S(1)} %get-tuple-element.7), channel_id=1, source_target_pairs={{4,0},{8,4},{12,8},{5,1},{9,5},{13,9},{6,2},{10,6},{14,10},{7,3},{... | collective-permute-start | bytes 1572872 | tf_op jit(solution)/shard_map/ppermute | solution.py:15
  9.9 5.6 %collective-permute-start = (bf16[2,16,16,512]{3,2,1,0:T(8,128)(2,1)S(1)}, bf16[2,16,16,512]{3,2,1,0:T(8,128)(2,1)S(1)}, u32[]{:S(2)}, u32[]{:S(2)}) collective-permute-start(bf16[2,16,16,512]{3,2,1,0:T(8,128)(2,1)S(1)} %get-tuple-element.8), channel_id=1, source_target_pairs={{0,4},{4,8},{8,12},{1,5},{5,9},{9,13},{2,6},{6,10},{10,14},{3,7},{... | collective-permute-start | bytes 1572872 | tf_op jit(solution)/shard_map/ppermute | solution.py:14
  16.3 17.7 %collective-permute-done = bf16[2,16,16,512]{3,2,1,0:T(8,128)(2,1)S(1)} collective-permute-done((bf16[2,16,16,512]{3,2,1,0:T(8,128)(2,1)S(1)}, bf16[2,16,16,512]{3,2,1,0:T(8,128)(2,1)S(1)}, u32[]{:S(2)}, u32[]{:S(2)}) %collective-permute-start) | collective-permute-done | bytes 524320 | tf_op jit(solution)/shard_map/ppermute | solution.py:14
  34.1 1.4 %copy-done.2 = bf16[8,16,16,512]{3,2,1,0:T(8,128)(2,1)} copy-done((bf16[8,16,16,512]{3,2,1,0:T(8,128)(2,1)}, bf16[8,16,16,512]{3,2,1,0:T(8,128)(2,1)S(1)}, u32[]{:S(2)}) %copy-start.2) | copy-done | bytes 2097176
  35.5 3.8 %collective-permute-start.2 = (bf16[8,2,16,512]{3,2,1,0:T(8,128)(2,1)S(1)}, bf16[8,2,16,512]{3,2,1,0:T(8,128)(2,1)S(1)}, u32[]{:S(2)}, u32[]{:S(2)}) collective-permute-start(bf16[8,2,16,512]{3,2,1,0:T(8,128)(2,1)S(1)} %get-tuple-element.5), channel_id=1, source_target_pairs={{0,2},{1,3},{4,6},{5,7},{8,10},{9,11},{12,14},{13,15},{16,18},{17,... | collective-permute-start | bytes 786440 | tf_op jit(solution)/shard_map/ppermute | solution.py:14
  39.3 1.3 %collective-permute-start.3 = (bf16[8,2,16,512]{3,2,1,0:T(8,128)(2,1)S(1)}, bf16[8,2,16,512]{3,2,1,0:T(8,128)(2,1)S(1)}, u32[]{:S(2)}, u32[]{:S(2)}) collective-permute-start(bf16[8,2,16,512]{3,2,1,0:T(8,128)(2,1)S(1)} %get-tuple-element.6), channel_id=1, source_target_pairs={{2,0},{3,1},{6,4},{7,5},{10,8},{11,9},{14,12},{15,13},{18,16},{19,... | collective-permute-start | bytes 786440 | tf_op jit(solution)/shard_map/ppermute | solution.py:15
  40.9 0.2 and.85
  41.1 2.1 %collective-permute-done.2 = bf16[8,2,16,512]{3,2,1,0:T(8,128)(2,1)S(1)} collective-permute-done((bf16[8,2,16,512]{3,2,1,0:T(8,128)(2,1)S(1)}, bf16[8,2,16,512]{3,2,1,0:T(8,128)(2,1)S(1)}, u32[]{:S(2)}, u32[]{:S(2)}) %collective-permute-start.2) | collective-permute-done | bytes 262176 | tf_op jit(solution)/shard_map/ppermute | solution.py:14
  43.2 4.4 %collective-permute-done.3 = bf16[8,2,16,512]{3,2,1,0:T(8,128)(2,1)S(1)} collective-permute-done((bf16[8,2,16,512]{3,2,1,0:T(8,128)(2,1)S(1)}, bf16[8,2,16,512]{3,2,1,0:T(8,128)(2,1)S(1)}, u32[]{:S(2)}, u32[]{:S(2)}) %collective-permute-start.3) | collective-permute-done | bytes 262176 | tf_op jit(solution)/shard_map/ppermute | solution.py:15
  47.6 1.9 %pad_maximum_fusion = bf16[8,20,16,512]{3,2,1,0:T(8,128)(2,1)S(1)} fusion(bf16[8,2,16,512]{3,2,1,0:T(8,128)(2,1)S(1)} %collective-permute-done.3, bf16[8,16,16,512]{3,2,1,0:T(8,128)(2,1)} %copy-done.2, bf16[8,2,16,512]{3,2,1,0:T(8,128)(2,1)S(1)} %collective-permute-done.2), kind=kLoop, calls=%fused_computation.3 | loop fusion | flops 2621440 | bytes 5242880 | tf_op jit(solution)/shard_map/concatenate | solution.py:16
  49.5 2.8 %gather_fusion = bf16[256,16,512]{2,1,0:T(8,128)(2,1)} fusion(bf16[160,16,512]{2,1,0:T(8,128)(2,1)S(1)} %bitcast.35, s32[1024]{0:T(1024)S(1)} %pad_clamp_fusion.1), kind=kCustom, calls=%fused_computation | custom fusion | bytes 8389632 | tf_op jit(solution)/shard_map/jit(_take)/gather | solution.py:31
  52.3 4.1 %broadcast_select_fusion = bf16[256,16,512]{2,1,0:T(8,128)(2,1)} fusion(bf16[256,16,512]{2,1,0:T(8,128)(2,1)} %gather_fusion, pred[256]{0:T(512)(128)(4,1)S(1)} %compare_and_fusion.2), kind=kLoop, calls=%fused_computation.2 | loop fusion | flops 2097152 | bytes 8388864 | tf_op jit(solution)/shard_map/jit(_take)/select_n | solution.py:31
  56.4 38.4 %all-gather.2.cloned.1.call-done = bf16[16,16,16,512]{3,2,1,0:T(8,128)(2,1)} async-done(((bf16[4,16,16,512]{3,2,1,0:T(8,128)(2,1)}), bf16[16,16,16,512]{3,2,1,0:T(8,128)(2,1)}) %all-gather.2.cloned.1.call-update) | async-done | bytes 4194320 | tf_op jit(solution)/shard_map/all_gather | solution.py:45
  94.8 2.9 %gather_fusion.1 = bf16[128,16,512]{2,1,0:T(8,128)(2,1)S(1)} fusion(bf16[256,16,512]{2,1,0:T(8,128)(2,1)} %bitcast.39, s32[1024]{0:T(1024)S(1)} %pad_clamp_fusion), kind=kCustom, calls=%fused_computation.1 | custom fusion | bytes 4194816 | tf_op jit(solution)/shard_map/jit(_take)/gather | solution.py:51
  97.7 0.7 select_select_fusion
  98.4 0.5 copy-done.8
  98.9 1.3 %fusion.2 = f32[64,16,512,1]{2,1,3,0:T(8,128)S(1)} fusion(bf16[64,2,16,512]{3,2,1,0:T(8,128)(2,1)S(1)} %bitcast.38, bf16[64,2,8,512]{3,2,1,0:T(8,128)(2,1)S(1)} %bitcast.42), kind=kOutput, calls=%fused_computation.10 | convolution fusion | flops 1073741824 | bytes 5242880 | tf_op jit(solution)/shard_map/dot_general | solution.py:54
  100.2 0.9 copy-done.3
  101.1 0.7 copy-done.7
  101.8 3.7 %bitcast_select_fusion = f32[64,16,512]{2,1,0:T(8,128)} fusion(f32[64,16,512,1]{2,1,3,0:T(8,128)S(1)} %fusion.2, bf16[64,4,16,512]{3,2,1,0:T(8,128)(2,1)S(1)} %bitcast.37, bf16[64,4,8,512]{3,2,1,0:T(8,128)(2,1)S(1)} %bitcast.41, pred[64]{0:T(512)(128)(4,1)S(1)} %eq.20), kind=kOutput, calls=%fused_computation.7 | convolution fusion | flops 2148007936 | bytes 10485824 | tf_op jit(solution)/shard_map/dot_general | solution.py:34
  105.5 11.9 %reduce-scatter.2.cloned.1.call-done = f32[64,8,512]{2,1,0:T(8,128)} async-done(((f32[64,16,512]{2,1,0:T(8,128)}), f32[64,8,512]{2,1,0:T(8,128)}) %reduce-scatter.2.cloned.1.call-update) | async-done | bytes 1048592 | tf_op jit(solution)/shard_map/reduce_scatter | solution.py:62
  117.4 2.2 %subtract_convert_fusion = bf16[64,8,512]{2,1,0:T(8,128)(2,1)} fusion(f32[64,8,512]{2,1,0:T(8,128)} %reduce-scatter.2.cloned.1.call-done, bf16[64,16,512]{2,1,0:T(8,128)(2,1)S(1)} %bitcast.36, s32[]{:T(128)S(6)} %select_n.123), kind=kLoop, calls=%fused_computation.12 | loop fusion | flops 786432 | bytes 2097156 | tf_op jit(solution)/shard_map/convert_element_type | solution.py:64
  (40 shorter events, 1.3 us)
Async XLA Ops:
  6.5 27.5 %copy-start = (bf16[4,16,16,512]{3,2,1,0:T(8,128)(2,1)S(1)}, bf16[4,16,16,512]{3,2,1,0:T(8,128)(2,1)}, u32[]{:S(2)}) copy-start(bf16[4,16,16,512]{3,2,1,0:T(8,128)(2,1)} %param.6) | copy-start | bytes 3145732
  6.5 9.0 %copy-start.4 = (s32[4,16,2]{1,2,0:T(2,128)S(1)}, s32[4,16,2]{1,2,0:T(2,128)}, u32[]{:S(2)}) copy-start(s32[4,16,2]{1,2,0:T(2,128)} %param.9) | copy-start | bytes 1540
  6.5 9.4 %copy-start.5 = (s32[4,16,4]{1,2,0:T(4,128)S(1)}, s32[4,16,4]{1,2,0:T(4,128)}, u32[]{:S(2)}) copy-start(s32[4,16,4]{1,2,0:T(4,128)} %param.8) | copy-start | bytes 3076
  6.5 9.7 %copy-start.6 = (s32[4,16]{1,0:T(4,128)S(1)}, s32[4,16]{1,0:T(4,128)}, u32[]{:S(2)}) copy-start(s32[4,16]{1,0:T(4,128)} %param.7) | copy-start | bytes 772
  6.5 88.3 %all-gather.2.cloned.1.call-start = ((), (), s32[]{:S(2)}) async-start(), calls=%async_computation.1 | async-start | bytes 5242880 | tf_op jit(solution)/shard_map/all_gather | solution.py:45
  7.3 110.2 %reduce-scatter.2.cloned.1.call-start = ((), (), s32[]{:S(2)}) async-start(), calls=%async_computation.2 | async-start | bytes 3145728 | tf_op jit(solution)/shard_map/reduce_scatter | solution.py:62
  8.6 25.5 %collective-permute-start.1 = (bf16[2,16,16,512]{3,2,1,0:T(8,128)(2,1)S(1)}, bf16[2,16,16,512]{3,2,1,0:T(8,128)(2,1)S(1)}, u32[]{:S(2)}, u32[]{:S(2)}) collective-permute-start(bf16[2,16,16,512]{3,2,1,0:T(8,128)(2,1)S(1)} %get-tuple-element.7), channel_id=1, source_target_pairs={{4,0},{8,4},{12,8},{5,1},{9,5},{13,9},{6,2},{10,6},{14,10},{7,3},{... | collective-permute-start | bytes 1572872 | tf_op jit(solution)/shard_map/ppermute | solution.py:15
  9.9 24.1 %collective-permute-start = (bf16[2,16,16,512]{3,2,1,0:T(8,128)(2,1)S(1)}, bf16[2,16,16,512]{3,2,1,0:T(8,128)(2,1)S(1)}, u32[]{:S(2)}, u32[]{:S(2)}) collective-permute-start(bf16[2,16,16,512]{3,2,1,0:T(8,128)(2,1)S(1)} %get-tuple-element.8), channel_id=1, source_target_pairs={{0,4},{4,8},{8,12},{1,5},{5,9},{9,13},{2,6},{6,10},{10,14},{3,7},{... | collective-permute-start | bytes 1572872 | tf_op jit(solution)/shard_map/ppermute | solution.py:14
  34.1 1.4 %copy-start.2 = (bf16[8,16,16,512]{3,2,1,0:T(8,128)(2,1)}, bf16[8,16,16,512]{3,2,1,0:T(8,128)(2,1)S(1)}, u32[]{:S(2)}) copy-start(bf16[8,16,16,512]{3,2,1,0:T(8,128)(2,1)S(1)} %constant_dynamic-update-slice_fusion) | copy-start | bytes 6291460
  35.5 7.6 %collective-permute-start.2 = (bf16[8,2,16,512]{3,2,1,0:T(8,128)(2,1)S(1)}, bf16[8,2,16,512]{3,2,1,0:T(8,128)(2,1)S(1)}, u32[]{:S(2)}, u32[]{:S(2)}) collective-permute-start(bf16[8,2,16,512]{3,2,1,0:T(8,128)(2,1)S(1)} %get-tuple-element.5), channel_id=1, source_target_pairs={{0,2},{1,3},{4,6},{5,7},{8,10},{9,11},{12,14},{13,15},{16,18},{17,... | collective-permute-start | bytes 786440 | tf_op jit(solution)/shard_map/ppermute | solution.py:14
  39.3 8.3 %collective-permute-start.3 = (bf16[8,2,16,512]{3,2,1,0:T(8,128)(2,1)S(1)}, bf16[8,2,16,512]{3,2,1,0:T(8,128)(2,1)S(1)}, u32[]{:S(2)}, u32[]{:S(2)}) collective-permute-start(bf16[8,2,16,512]{3,2,1,0:T(8,128)(2,1)S(1)} %get-tuple-element.6), channel_id=1, source_target_pairs={{2,0},{3,1},{6,4},{7,5},{10,8},{11,9},{14,12},{15,13},{18,16},{19,... | collective-permute-start | bytes 786440 | tf_op jit(solution)/shard_map/ppermute | solution.py:15
  97.7 1.2 copy-start.8
  98.9 2.2 %copy-start.3 = (bf16[256,16,512]{2,1,0:T(8,128)(2,1)S(1)}, bf16[256,16,512]{2,1,0:T(8,128)(2,1)}, u32[]{:S(2)}) copy-start(bf16[256,16,512]{2,1,0:T(8,128)(2,1)} %broadcast_select_fusion) | copy-start | bytes 12582916
  98.9 2.9 %copy-start.7 = (bf16[512,2048]{1,0:T(8,128)(2,1)S(1)}, bf16[512,2048]{1,0:T(8,128)(2,1)}, u32[]{:S(2)}) copy-start(bf16[512,2048]{1,0:T(8,128)(2,1)} %param.10) | copy-start | bytes 6291460
  105.5 11.9 %copy-start.1 = (bf16[4,16,16,512]{3,2,1,0:T(8,128)(2,1)S(1)}, bf16[4,16,16,512]{3,2,1,0:T(8,128)(2,1)}, u32[]{:S(2)}) copy-start(bf16[4,16,16,512]{3,2,1,0:T(8,128)(2,1)} %param.6) | copy-start | bytes 3145732
Sparse Core Ops, SparseCore 0:
  8.9 85.8 all-gather.1
  105.7 11.7 reduce-scatter.1
where the time goes:
time: 127 us; the launch traced here: 126 us
  waiting for transfers between devices  75.2 us (59%)
  between operations  13.6 us (11%)
  starting transfers between devices  12 us (9%)
  local copies, waits for them, and re-layouts  11.6 us (9%)
  other arithmetic  9.03 us (7%)
  matrix products  4.99 us (4%)
    all_gather x1, waiting for transfers between devices, on_device(): piece = lax.all_gather(convergence, 'rows', axis=0, tiled=True)  38.4 us
    ppermute x2, waiting for transfers between devices, padded(): before = lax.ppermute(last, axis, up)  19.7 us
    reduce_scatter x1, waiting for transfers between devices, on_device(): lax.psum_scatter(partial_value, 'sub', scatter_dimension=1, tiled=True)  11.9 us
    ppermute x2, starting transfers between devices, padded(): before = lax.ppermute(last, axis, up)  9.39 us
    ppermute x2, waiting for transfers between devices, padded(): after = lax.ppermute(first, axis, down)  4.41 us
    select_n x2, other arithmetic, on_device(): jnp.take(flat_ext, near_index.reshape(-1), axis=0)  4.1 us
    dot_general x1, matrix products, on_device(): lax.dot_general(near_blocks, near_factor.reshape(pixels, near_slots, pixe...  3.7 us
    unnamed x20, local copies, waits for them, and re-layouts  3.55 us
  transfers between devices with their start and end apart: 6, of which 5 were waited for; matrix products, arithmetic and copies ran while one was open for 9% of the time, Pallas kernels for 0%

commit v1 on v0

v1 whole, which is shorter than its diff:
```python
import functools

import jax
import jax.numpy as jnp
from jax import lax
from jax.experimental import pallas as pl
from jax.experimental.pallas import tpu as pltpu
from jax.sharding import PartitionSpec as P

MESH = pl.DeviceIdType.MESH
CHUNKS = 4
ROW_STRIDE_BITS = 8


def kernel(dims, conv, codes, near_factor, far_factor, out, *scratch):
    n_rows, n_cols, tile_rows, tile_cols, half, pixels, near_slots, far_slots, chunks = dims
    chunk_cols = tile_cols // chunks
    far = scratch[:chunks]
    (near, near_w, far_w, codes_v, codes_s, near_g, far_g, near_acc, far_acc,
     white_src, white_dst, tile_send, tile_recv, white_send, white_recv,
     side_send, side_recv, code_send, code_recv, fac_send, fac_recv, loc_sem, halo_sem) = scratch[chunks:]

    i = lax.axis_index("rows")
    x = lax.axis_index("cols")
    s = lax.axis_index("sub")
    other = 1 - s
    mine = pl.ds(pl.multiple_of(s * half, half), half)
    is_end = (i == 0) | (i == n_rows - 1)
    is_mid = (i > 0) & (i < n_rows - 1)
    low_helper = i == 1
    high_helper = i == n_rows - 2
    is_helper = low_helper | high_helper
    end_tile = jnp.where(low_helper, 0, n_rows - 1)
    to_mid = jnp.where(i == 0, 1, n_rows - 2)

    def cols_of(k):
        return pl.ds(k * chunk_cols, chunk_cols)

    local = [
        pltpu.make_async_copy(
            conv.at[:, :, mine, :],
            near.at[pl.ds(2, tile_rows), pl.ds(2, tile_cols)],
            loc_sem.at[0],
        ),
        pltpu.make_async_copy(near_factor, near_w.at[s], loc_sem.at[1]),
        pltpu.make_async_copy(far_factor, far_w.at[s], loc_sem.at[2]),
        pltpu.make_async_copy(codes, codes_s.at[0, s], loc_sem.at[3]),
    ]
    for copy in local:
        copy.start()
    own_far = [
        pltpu.make_async_copy(
            conv.at[:, cols_of(k), mine, :],
            far[k].at[pl.ds(i * tile_rows, tile_rows)],
            loc_sem.at[6 + k],
        )
        for k in range(chunks)
    ]

    @pl.when(is_mid)
    def _():
        for copy in own_far:
            copy.start()

    @pl.when(i == 0)
    def _():
        near[0:2] = jnp.zeros((2,) + near.shape[1:], near.dtype)

    @pl.when(i == n_rows - 1)
    def _():
        near[tile_rows + 2:tile_rows + 4] = jnp.zeros((2,) + near.shape[1:], near.dtype)

    @pl.when(x == 0)
    def _():
        near[:, 0:2] = jnp.zeros((near.shape[0], 2) + near.shape[2:], near.dtype)

    @pl.when(x == n_cols - 1)
    def _():
        near[:, tile_cols + 2:tile_cols + 4] = jnp.zeros((near.shape[0], 2) + near.shape[2:], near.dtype)

    barrier = pltpu.get_barrier_semaphore()
    offsets = [(di, dx) for di in (-1, 0, 1) for dx in (-1, 0, 1) if (di, dx) != (0, 0)]

    def present(di, dx):
        ok = jnp.bool_(True)
        if di == -1:
            ok = ok & (i > 0)
        if di == 1:
            ok = ok & (i < n_rows - 1)
        if dx == -1:
            ok = ok & (x > 0)
        if dx == 1:
            ok = ok & (x < n_cols - 1)
        return ok

    for di, dx in offsets:
        @pl.when(present(di, dx))
        def _():
            pl.semaphore_signal(barrier, inc=1, device_id={"rows": i + di, "cols": x + dx}, device_id_type=MESH)
    for di in (-1, 0, 1):
        @pl.when(present(di, 0))
        def _():
            pl.semaphore_signal(barrier, inc=1, device_id={"rows": i + di, "sub": other}, device_id_type=MESH)
    count_z = (i > 0).astype(jnp.int32) + (i < n_rows - 1).astype(jnp.int32) + 1
    count_x = (x > 0).astype(jnp.int32) + (x < n_cols - 1).astype(jnp.int32) + 1
    pl.semaphore_wait(barrier, count_z * count_x - 1 + count_z)

    def code_copy(which, slot, target):
        return pltpu.make_async_remote_copy(
            src_ref=codes, dst_ref=codes_v.at[slot, s], send_sem=code_send.at[which],
            recv_sem=code_recv.at[which], device_id=target, device_id_type=MESH)

    code_partner = code_copy(0, 0, {"sub": other})
    code_straight = code_copy(1, 1, {"rows": to_mid})
    code_cross = code_copy(2, 1, {"rows": to_mid, "sub": other})
    code_partner.start()

    @pl.when(is_end)
    def _():
        code_straight.start()
        code_cross.start()

    def side_copy(di, dx):
        if di == 0:
            rows_src, rows_dst = pl.ds(0, tile_rows), pl.ds(2, tile_rows)
        elif di == -1:
            rows_src, rows_dst = pl.ds(0, 2), pl.ds(tile_rows + 2, 2)
        else:
            rows_src, rows_dst = pl.ds(tile_rows - 2, 2), pl.ds(0, 2)
        if dx == 0:
            cols_src, cols_dst = pl.ds(0, tile_cols), pl.ds(2, tile_cols)
        elif dx == -1:
            cols_src, cols_dst = pl.ds(0, 2), pl.ds(tile_cols + 2, 2)
        else:
            cols_src, cols_dst = pl.ds(tile_cols - 2, 2), pl.ds(0, 2)
        which = offsets.index((di, dx))
        return pltpu.make_async_remote_copy(
            src_ref=conv.at[rows_src, cols_src, mine, :],
            dst_ref=near.at[rows_dst, cols_dst],
            send_sem=side_send.at[which], recv_sem=side_recv.at[which],
            device_id={"rows": i + di, "cols": x + dx}, device_id_type=MESH)

    def side_sends(di, dx):
        if dx == 0:
            return low_helper if di == -1 else high_helper
        return present(di, dx)

    def side_receives(di, dx):
        if dx == 0:
            return (i == 0) if di == -1 else (i == n_rows - 1)
        return present(-di, -dx)

    def tile_copy(way, d, k, tile):
        src = conv.at[:, cols_of(k), mine, :] if d == 0 else far[k].at[pl.ds(tile * tile_rows, tile_rows)]
        return pltpu.make_async_remote_copy(
            src_ref=src, dst_ref=far[k].at[pl.ds(tile * tile_rows, tile_rows)],
            send_sem=tile_send.at[way, d, k], recv_sem=tile_recv.at[way, d, k],
            device_id={"rows": i - 1 if way == 0 else i + 1}, device_id_type=MESH)

    def sent(way, d, k):
        return tile_copy(way, d, k, i + d if way == 0 else i - d)

    def received(way, d, k):
        return tile_copy(way, d, k, i + 1 + d if way == 0 else i - 1 - d)

    def tile_sends(way, d):
        if way == 0:
            return (i >= 2) & (i + d <= n_rows - 1)
        return (i <= n_rows - 3) & (i - d >= 0)

    def tile_receives(way, d):
        if way == 0:
            return is_mid & (i + 1 + d <= n_rows - 1)
        return is_mid & (i - 1 - d >= 0)

    for k in range(chunks):
        for way in (0, 1):
            @pl.when(tile_sends(way, 0))
            def _():
                sent(way, 0, k).start()
        if k == 0:
            for di, dx in offsets:
                @pl.when(side_sends(di, dx))
                def _():
                    side_copy(di, dx).start()

    def factor_copy(which):
        src, dst = ((near_factor, near_w), (far_factor, far_w))[which]
        return pltpu.make_async_remote_copy(
            src_ref=src, dst_ref=dst.at[s], send_sem=fac_send.at[which],
            recv_sem=fac_recv.at[which], device_id={"sub": other}, device_id_type=MESH)

    for which in (0, 1):
        factor_copy(which).start()

    def halo_copy(way, k):
        if way == 0:
            src_rows, dst_rows = pl.ds((i + 1) * tile_rows, 2), pl.ds(tile_rows + 2, 2)
        else:
            src_rows, dst_rows = pl.ds(i * tile_rows - 2, 2), pl.ds(0, 2)
        return pltpu.make_async_copy(
            far[k].at[src_rows], near.at[dst_rows, pl.ds(2 + k * chunk_cols, chunk_cols)], halo_sem.at[way, k])

    for d in range(n_rows - 3):
        for k in range(chunks):
            for way in (0, 1):
                @pl.when(tile_receives(way, d))
                def _():
                    received(way, d, k).wait_recv()
                    if d == 0:
                        halo_copy(way, k).start()

                @pl.when(tile_sends(way, d + 1))
                def _():
                    sent(way, d + 1, k).start()

    code_copy(0, 0, {"sub": other}).wait_recv()
    code_in = pltpu.make_async_copy(codes_v.at[0, other], codes_s.at[0, other], loc_sem.at[4])
    code_in.start()
    end_codes = pltpu.make_async_copy(codes_v.at[1], codes_s.at[1], loc_sem.at[5])

    @pl.when(is_helper)
    def _():
        code_straight.wait_recv()
        code_cross.wait_recv()
        end_codes.start()
        end_codes.wait()

    code_in.wait()
    for copy in local:
        copy.wait()
    for which in (0, 1):
        factor_copy(which).wait_recv()

    @pl.when(is_mid)
    def _():
        for k in range(chunks):
            halo_copy(0, k).wait()
            halo_copy(1, k).wait()
            own_far[k].wait()

    for di, dx in offsets:
        @pl.when(side_receives(di, dx))
        def _():
            side_copy(di, dx).wait_recv()

    pairs = tile_cols // 2

    def gather_near(t, carry):
        r = t // pairs
        c = (t % pairs) * 2
        at = pl.ds(pl.multiple_of(t * 2 * half, 2 * half), 2 * half)
        for sub in range(2):
            for slot in range(near_slots):
                parts = []
                for step in range(2):
                    place = codes_s[0, sub, r, (c + step) * near_slots + slot]
                    row = lax.shift_right_logical(place, ROW_STRIDE_BITS)
                    col = place & ((1 << ROW_STRIDE_BITS) - 1)
                    parts.append(near[row, col].astype(jnp.float32))
                near_g[sub * near_slots + slot, at, :] = jnp.concatenate(parts, axis=0).astype(jnp.bfloat16)
        return carry

    lax.fori_loop(0, tile_rows * pairs, gather_near, 0)
    contract = (((1,), (1,)), ((), ()))

    def near_dot(first, sub, slot):
        where = pl.ds(pl.multiple_of(slot * pixels, pixels), pixels)
        product = lax.dot_general(
            near_g[sub * near_slots + slot], near_w[sub, :, where], contract, preferred_element_type=jnp.float32)
        if first:
            near_acc[...] = product
        else:
            near_acc[...] += product

    near_dot(True, 0, 0)

    def near_step(t, carry):
        near_dot(False, t // near_slots, t % near_slots)
        return carry

    lax.fori_loop(1, 2 * near_slots, near_step, 0)

    level_at = tile_cols * (near_slots + far_slots)
    far_at = tile_cols * near_slots
    chunk_blocks = tile_rows * chunk_cols
    chunk_rows = chunk_blocks * half

    def block_rows(block):
        return pl.ds(pl.multiple_of(block * half, half), half)

    def far_chunk(k):
        def gather_far(who, base):
            def body(t, carry):
                at = pl.ds(pl.multiple_of(base + t * 2 * half, 2 * half), 2 * half)
                for sub in range(2):
                    for slot in range(far_slots):
                        parts = []
                        for step in range(2):
                            block = 2 * t + step
                            r, c = block // chunk_cols, block % chunk_cols
                            row = codes_s[who, sub, r, far_at + (k * chunk_cols + c) * far_slots + slot]
                            parts.append(far[k][row, c].astype(jnp.float32))
                        far_g[sub * far_slots + slot, at, :] = jnp.concatenate(parts, axis=0).astype(jnp.bfloat16)
                return carry

            lax.fori_loop(0, chunk_blocks // 2, body, 0)

        gather_far(0, 0)

        @pl.when(is_helper)
        def _():
            gather_far(1, chunk_rows)

        for sub in range(2):
            for slot in range(far_slots):
                product = lax.dot_general(
                    far_g[sub * far_slots + slot], far_w[sub, :, slot * pixels:(slot + 1) * pixels],
                    contract, preferred_element_type=jnp.float32)
                if sub + slot == 0:
                    far_acc[...] = product
                else:
                    far_acc[...] += product

        @pl.when(is_helper)
        def _():
            def body(block, carry):
                r, c = block // chunk_cols, block % chunk_cols
                value = far[k][end_tile * tile_rows + r, c].astype(jnp.float32)
                mean = far_acc[block_rows(chunk_blocks + block), :]
                white_src[r, k * chunk_cols + c] = (value - mean).astype(jnp.bfloat16)
                return carry

            lax.fori_loop(0, chunk_blocks, body, 0)
            white_copy(k).start()

        def body(block, carry):
            r, c = block // chunk_cols, block % chunk_cols
            col = k * chunk_cols + c
            level = codes_s[0, 0, r, level_at + col]
            mean = jnp.where(level == 1, near_acc[block_rows(r * tile_cols + col), :], far_acc[block_rows(block), :])
            out[r, col] = (near[2 + r, 2 + col].astype(jnp.float32) - mean).astype(jnp.bfloat16)
            return carry

        lax.fori_loop(0, chunk_blocks, body, 0)

    def white_copy(k):
        return pltpu.make_async_remote_copy(
            src_ref=white_src.at[:, cols_of(k)], dst_ref=white_dst.at[:, cols_of(k)],
            send_sem=white_send.at[k], recv_sem=white_recv.at[k],
            device_id={"rows": end_tile}, device_id_type=MESH)

    @pl.when(is_mid)
    def _():
        for k in range(chunks):
            d = n_rows - 3
            for way in (0, 1):
                @pl.when(tile_receives(way, d))
                def _():
                    received(way, d, k).wait_recv()
            far_chunk(k)

    @pl.when(is_end)
    def _():
        for k in range(chunks):
            white_copy(k).wait_recv()

            def body(block, carry):
                r, c = block // chunk_cols, block % chunk_cols
                col = k * chunk_cols + c
                level = codes_s[0, 0, r, level_at + col]
                fine = near[2 + r, 2 + col].astype(jnp.float32) - near_acc[block_rows(r * tile_cols + col), :]
                coarse = white_dst[r, col].astype(jnp.float32)
                out[r, col] = jnp.where(level == 1, fine, coarse).astype(jnp.bfloat16)
                return carry

            lax.fori_loop(0, chunk_blocks, body, 0)

    code_partner.wait_send()

    @pl.when(is_end)
    def _():
        code_straight.wait_send()
        code_cross.wait_send()

    for di, dx in offsets:
        @pl.when(side_sends(di, dx))
        def _():
            side_copy(di, dx).wait_send()
    for which in (0, 1):
        factor_copy(which).wait_send()
    for d in range(n_rows - 2):
        for way in (0, 1):
            @pl.when(tile_sends(way, d))
            def _():
                for k in range(chunks):
                    sent(way, d, k).wait_send()

    @pl.when(is_helper)
    def _():
        for k in range(chunks):
            white_copy(k).wait_send()


def on_device(convergence, block_level, near_codes, far_rows, near_factor, far_factor):
    tile_rows, tile_cols, samples, pixels = convergence.shape
    n_rows, n_cols = lax.axis_size("rows"), lax.axis_size("cols")
    near_slots, far_slots = near_codes.shape[2], far_rows.shape[2]
    half = samples // 2
    chunks = CHUNKS
    chunk_cols = tile_cols // chunks
    row_pos = jnp.arange(tile_rows, dtype=jnp.int32)[:, None, None]
    col_pos = jnp.arange(tile_cols, dtype=jnp.int32)[None, :, None]
    places = (row_pos + near_codes // 5) * (1 << ROW_STRIDE_BITS) + col_pos + near_codes % 5
    codes = jnp.concatenate(
        [places.reshape(tile_rows, -1), far_rows.reshape(tile_rows, -1), block_level], axis=1)
    width = codes.shape[1]
    codes = jnp.pad(codes, ((0, 0), (0, -width % 128)))
    dims = (n_rows, n_cols, tile_rows, tile_cols, half, pixels, near_slots, far_slots, chunks)
    block = (half, pixels)
    bf16, f32 = jnp.bfloat16, jnp.float32
    chunk_rows = tile_rows * chunk_cols * half
    dma = pltpu.SemaphoreType.DMA
    scratch = [pltpu.VMEM((n_rows * tile_rows, chunk_cols) + block, bf16) for _ in range(chunks)]
    scratch += [
        pltpu.VMEM((tile_rows + 4, tile_cols + 4) + block, bf16),
        pltpu.VMEM((2,) + near_factor.shape, bf16),
        pltpu.VMEM((2,) + far_factor.shape, bf16),
        pltpu.VMEM((2, 2) + codes.shape, jnp.int32),
        pltpu.SMEM((2, 2) + codes.shape, jnp.int32),
        pltpu.VMEM((2 * near_slots, tile_rows * tile_cols * half, pixels), bf16),
        pltpu.VMEM((2 * far_slots, 2 * chunk_rows, pixels), bf16),
        pltpu.VMEM((tile_rows * tile_cols * half, pixels), f32),
        pltpu.VMEM((2 * chunk_rows, pixels), f32),
        pltpu.VMEM((tile_rows, tile_cols) + block, bf16),
        pltpu.VMEM((tile_rows, tile_cols) + block, bf16),
        dma((2, n_rows - 2, chunks)),
        dma((2, n_rows - 2, chunks)),
        dma((chunks,)),
        dma((chunks,)),
        dma((8,)),
        dma((8,)),
        dma((3,)),
        dma((3,)),
        dma((2,)),
        dma((2,)),
        dma((6 + chunks,)),
        dma((2, chunks)),
    ]
    anywhere = pl.BlockSpec(memory_space=pl.ANY)
    vmem = pl.BlockSpec(memory_space=pltpu.VMEM)
    return pl.pallas_call(
        functools.partial(kernel, dims),
        out_shape=jax.ShapeDtypeStruct((tile_rows, tile_cols) + block, bf16),
        in_specs=[anywhere, vmem, anywhere, anywhere],
        out_specs=vmem,
        scratch_shapes=scratch,
        compiler_params=pltpu.CompilerParams(
            collective_id=0, has_side_effects=True, vmem_limit_bytes=56 * 1024 * 1024),
    )(convergence, codes, near_factor, far_factor)


def solution(mesh):
    placed = (
        P(("fields", "rows"), "cols", None, None),
        P(("fields", "rows"), "cols"),
        P(("fields", "rows"), "cols", "sub"),
        P(("fields", "rows"), "cols", "sub"),
        P(None, "sub"),
        P(None, "sub"),
    )
    return jax.shard_map(
        on_device,
        mesh=mesh,
        in_specs=placed,
        out_specs=P(("fields", "rows"), "cols", "sub", None),
        check_vma=False,
    )
```

time: 127 us -> 47.4 us (0.37)
  waiting for transfers between devices: 75.2 us -> 0 us
  Pallas kernels: 0 us -> 42.1 us
  between operations: 13.6 us -> 0.02 us
  starting transfers between devices: 12 us -> 0 us
  local copies, waits for them, and re-layouts: 11.6 us -> 3.5 us
  other arithmetic: 9.03 us -> 1.48 us
  matrix products: 4.99 us -> 0 us
    pallas_call x0 -> x1, Pallas kernels: none -> 42.1 us  [on_device(): pl.pallas_call(functools.partial(kernel, dims), out_shape=jax.ShapeDtypeS...]
    all_gather x1 -> x0, waiting for transfers between devices: 38.4 us -> none  [on_device(): piece = lax.all_gather(convergence, 'rows', axis=0, tiled=True)]
    ppermute x4 -> x0, waiting for transfers between devices: 24.1 us -> none  [the longest x2 19.7 us: padded(): before = lax.ppermute(last, axis, up)]
    ppermute x4 -> x0, starting transfers between devices: 12 us -> none  [the longest x2 9.39 us: padded(): before = lax.ppermute(last, axis, up)]
    reduce_scatter x1 -> x0, waiting for transfers between devices: 11.9 us -> none  [on_device(): lax.psum_scatter(partial_value, 'sub', scatter_dimension=1, tiled=True)]
    gather x2 -> x0, local copies, waits for them, and re-layouts: 5.68 us -> none  [the longest x1 2.87 us: on_device(): found = jnp.take(flat_piece, local, axis=0)]
    dot_general x2 -> x0, matrix products: 4.99 us -> none  [the longest x1 3.7 us: on_device(): lax.dot_general(near_blocks, near_factor.reshape(pixels, near_slots, pixe...]
    select_n x4 -> x0, other arithmetic: 4.83 us -> none  [the longest x2 4.1 us: on_device(): jnp.take(flat_ext, near_index.reshape(-1), axis=0)]
  transfers between devices with their start and end apart: 6 -> 0, of which waited for: 5 -> 0; matrix products, arithmetic and copies ran while one was open for 9% -> 0% of each run, Pallas kernels for 0% -> 0%
where the time goes in v1:
time: 47.4 us; the launch traced here: 47.1 us
  Pallas kernels  42.1 us (89%)
  local copies, waits for them, and re-layouts  3.5 us (7%)
  other arithmetic  1.48 us (3%)
    pallas_call x1, Pallas kernels, on_device(): pl.pallas_call(functools.partial(kernel, dims), out_shape=jax.ShapeDtypeS...  42.1 us
    unnamed x2, local copies, waits for them, and re-layouts  2.65 us

profile of v1, /device:TPU:0, one launch (start us, length us, event | category | flops | bytes accessed | tf_op | source)
XLA Modules:
  0.0 47.1 jit_solution(4768275750070190651)
XLA Ops:
  0.0 0.7 %fusion.1 = s32[4,16,4]{1,2,0:T(4,128)S(1)} fusion(s32[4,16,4]{1,2,0:T(4,128)} %param.8), kind=kLoop, calls=%fused_computation.3 | loop fusion | flops 4096 | bytes 2048 | tf_op jit(solution)/shard_map/add | solution.py:414
  0.7 0.8 %copy.11 = s32[4,16,2]{0,2,1:T(2,128)S(1)} copy(s32[4,16,2]{1,2,0:T(2,128)} %param.9) | data formatting | bytes 1024 | tf_op args[3]
  1.5 0.1 copy.12
  1.6 0.1 copy.10
  1.7 0.1 reshape.6
  1.8 0.8 %pad_add_fusion = s32[4,112]{1,0:T(4,128)S(1)} fusion(s32[4,16]{1,0:T(4,128)} %param.7, s32[4,32]{1,0:T(4,128)S(1)} %copy.12, s32[4,64]{1,0:T(4,128)S(1)} %reshape.6), kind=kLoop, calls=%fused_computation.7 | loop fusion | flops 896 | bytes 3584 | tf_op jit(solution)/shard_map/concatenate | solution.py:415
  2.5 0.6 %pad.4.codes = s32[4,128]{1,0:T(4,128)} pad(s32[4,112]{1,0:T(4,128)S(1)} %pad_add_fusion, s32[]{:T(128)} %constant.20.clone.1), padding=0_0x0_16 | pad | bytes 3844 | tf_op jit(solution)/shard_map/jit(_pad)/pad | solution.py:418
  3.1 42.1 %shard_map.64 = bf16[4,16,8,512]{3,2,1,0:T(8,128)(2,1)} custom-call(bf16[4,16,16,512]{3,2,1,0:T(8,128)(2,1)} %conv.1, s32[4,128]{1,0:T(4,128)} %pad.4.codes, bf16[512,2048]{1,0:T(8,128)(2,1)} %near_factor.1, bf16[512,1024]{1,0:T(8,128)(2,1)} %far_factor.1), custom_call_target="tpu_custom_call" | custom-call | tf_op jit(solution)/shard_map/pallas_call | solution.py:452
  45.2 1.9 %copy.14 = bf16[4,16,8,512]{3,2,1,0:T(8,128)(2,1)} copy(bf16[4,16,8,512]{3,2,1,0:T(8,128)(2,1)} %shard_map.64) | data formatting | bytes 1048576

commit v2 on v1

--- a/solution.py
+++ b/solution.py
@@ -8,17 +8,22 @@
 from jax.sharding import PartitionSpec as P
 
 MESH = pl.DeviceIdType.MESH
-CHUNKS = 4
-ROW_STRIDE_BITS = 8
+PARTS = 4
+
+
+def chunk_starts(cols):
+    return [0, cols * 5 // 16, cols * 10 // 16, cols * 14 // 16, cols]
 
 
 def kernel(dims, conv, codes, near_factor, far_factor, out, *scratch):
-    n_rows, n_cols, tile_rows, tile_cols, half, pixels, near_slots, far_slots, chunks = dims
-    chunk_cols = tile_cols // chunks
+    n_rows, n_cols, tile_rows, tile_cols, half, pixels, near_slots, far_slots = dims
+    starts = chunk_starts(tile_cols)
+    chunks = len(starts) - 1
+    sizes = [starts[k + 1] - starts[k] for k in range(chunks)]
     far = scratch[:chunks]
-    (near, near_w, far_w, codes_v, codes_s, near_g, far_g, near_acc, far_acc,
+    (near, near_w, far_w, codes_v, codes_s, near_g, far_g, near_acc, far_acc, end_acc,
      white_src, white_dst, tile_send, tile_recv, white_send, white_recv,
-     side_send, side_recv, code_send, code_recv, fac_send, fac_recv, loc_sem, halo_sem) = scratch[chunks:]
+     side_send, side_recv, corner_send, corner_recv, code_send, code_recv, fac_send, fac_recv, loc_sem, halo_sem) = scratch[chunks:]
 
     i = lax.axis_index("rows")
     x = lax.axis_index("cols")
@@ -34,7 +39,7 @@
     to_mid = jnp.where(i == 0, 1, n_rows - 2)
 
     def cols_of(k):
-        return pl.ds(k * chunk_cols, chunk_cols)
+        return pl.ds(starts[k], sizes[k])
 
     local = [
         pltpu.make_async_copy(
@@ -79,7 +84,7 @@
         near[:, tile_cols + 2:tile_cols + 4] = jnp.zeros((near.shape[0], 2) + near.shape[2:], near.dtype)
 
     barrier = pltpu.get_barrier_semaphore()
-    offsets = [(di, dx) for di in (-1, 0, 1) for dx in (-1, 0, 1) if (di, dx) != (0, 0)]
+    offsets = [(-1, 0), (1, 0), (0, -1), (0, 1)]
 
     def present(di, dx):
         ok = jnp.bool_(True)
@@ -97,28 +102,24 @@
         @pl.when(present(di, dx))
         def _():
             pl.semaphore_signal(barrier, inc=1, device_id={"rows": i + di, "cols": x + dx}, device_id_type=MESH)
-    for di in (-1, 0, 1):
-        @pl.when(present(di, 0))
-        def _():
-            pl.semaphore_signal(barrier, inc=1, device_id={"rows": i + di, "sub": other}, device_id_type=MESH)
-    count_z = (i > 0).astype(jnp.int32) + (i < n_rows - 1).astype(jnp.int32) + 1
-    count_x = (x > 0).astype(jnp.int32) + (x < n_cols - 1).astype(jnp.int32) + 1
-    pl.semaphore_wait(barrier, count_z * count_x - 1 + count_z)
+    pl.semaphore_signal(barrier, inc=1, device_id={"sub": other}, device_id_type=MESH)
+    count_z = (i > 0).astype(jnp.int32) + (i < n_rows - 1).astype(jnp.int32)
+    count_x = (x > 0).astype(jnp.int32) + (x < n_cols - 1).astype(jnp.int32)
+    pl.semaphore_wait(barrier, count_z + count_x + 1)
 
     def code_copy(which, slot, target):
         return pltpu.make_async_remote_copy(
-            src_ref=codes, dst_ref=codes_v.at[slot, s], send_sem=code_send.at[which],
-            recv_sem=code_recv.at[which], device_id=target, device_id_type=MESH)
+            src_ref=codes if which < 2 else codes_v.at[slot, s], dst_ref=codes_v.at[slot, s],
+            send_sem=code_send.at[which], recv_sem=code_recv.at[which], device_id=target, device_id_type=MESH)
 
     code_partner = code_copy(0, 0, {"sub": other})
     code_straight = code_copy(1, 1, {"rows": to_mid})
-    code_cross = code_copy(2, 1, {"rows": to_mid, "sub": other})
+    code_relay = code_copy(2, 1, {"sub": other})
     code_partner.start()
 
     @pl.when(is_end)
     def _():
         code_straight.start()
-        code_cross.start()
 
     def side_copy(di, dx):
         if di == 0:
@@ -199,7 +200,7 @@
         else:
             src_rows, dst_rows = pl.ds(i * tile_rows - 2, 2), pl.ds(0, 2)
         return pltpu.make_async_copy(
-            far[k].at[src_rows], near.at[dst_rows, pl.ds(2 + k * chunk_cols, chunk_cols)], halo_sem.at[way, k])
+            far[k].at[src_rows], near.at[dst_rows, pl.ds(2 + starts[k], sizes[k])], halo_sem.at[way, k])
 
     for d in range(n_rows - 3):
         for k in range(chunks):
@@ -222,15 +223,10 @@
     @pl.when(is_helper)
     def _():
         code_straight.wait_recv()
-        code_cross.wait_recv()
-        end_codes.start()
-        end_codes.wait()
-
-    code_in.wait()
+        code_relay.start()
+
     for copy in local:
         copy.wait()
-    for which in (0, 1):
-        factor_copy(which).wait_recv()
 
     @pl.when(is_mid)
     def _():
@@ -244,105 +240,117 @@
         def _():
             side_copy(di, dx).wait_recv()
 
-    pairs = tile_cols // 2
-
-    def gather_near(t, carry):
-        r = t // pairs
-        c = (t % pairs) * 2
-        at = pl.ds(pl.multiple_of(t * 2 * half, 2 * half), 2 * half)
-        for sub in range(2):
-            for slot in range(near_slots):
-                parts = []
-                for step in range(2):
-                    place = codes_s[0, sub, r, (c + step) * near_slots + slot]
-                    row = lax.shift_right_logical(place, ROW_STRIDE_BITS)
-                    col = place & ((1 << ROW_STRIDE_BITS) - 1)
-                    parts.append(near[row, col].astype(jnp.float32))
-                near_g[sub * near_slots + slot, at, :] = jnp.concatenate(parts, axis=0).astype(jnp.bfloat16)
-        return carry
-
-    lax.fori_loop(0, tile_rows * pairs, gather_near, 0)
+    def corner_copy(di, dx):
+        rows = pl.ds(0, 2) if di == -1 else pl.ds(tile_rows + 2, 2)
+        src, dst = (2, tile_cols + 2) if dx == -1 else (tile_cols, 0)
+        which = (di + 1) + (dx + 1) // 2
+        return pltpu.make_async_remote_copy(
+            src_ref=near.at[rows, pl.ds(src, 2)], dst_ref=near.at[rows, pl.ds(dst, 2)],
+            send_sem=corner_send.at[which], recv_sem=corner_recv.at[which],
+            device_id={"cols": x + dx}, device_id_type=MESH)
+
+    corners = [(di, dx) for di in (-1, 1) for dx in (-1, 1)]
+    for di, dx in corners:
+        @pl.when(present(di, 0) & present(0, dx))
+        def _():
+            corner_copy(di, dx).start()
+
+    @pl.when(is_helper)
+    def _():
+        code_relay.wait_recv()
+        end_codes.start()
+        end_codes.wait()
+
+    code_in.wait()
+    for which in (0, 1):
+        factor_copy(which).wait_recv()
+    for di, dx in corners:
+        @pl.when(present(di, 0) & present(0, -dx))
+        def _():
+            corner_copy(di, dx).wait_recv()
+
     contract = (((1,), (1,)), ((), ()))
-
-    def near_dot(first, sub, slot):
-        where = pl.ds(pl.multiple_of(slot * pixels, pixels), pixels)
+    part_slots = 2 * near_slots // PARTS
+
+    def block_rows(block):
+        return pl.ds(pl.multiple_of(block * half, half), half)
+
+    def pair_rows(block):
+        return pl.ds(pl.multiple_of(block * half, 2 * half), 2 * half)
+
+    def joined(first, second):
+        both = jnp.concatenate([first.astype(jnp.float32), second.astype(jnp.float32)], axis=0)
+        return both.astype(jnp.bfloat16)
+
+    def near_part(part):
+        sub, base = part * part_slots // near_slots, part * part_slots % near_slots
+
+        def near_block(r, c, slot):
+            code = codes_s[0, sub, r, base + slot, c]
+            down = lax.shift_right_logical(code * 205, 10)
+            return near[r + down, c + code - 5 * down]
+
+        def gather(c, carry):
+            for r in range(0, tile_rows, 2):
+                for slot in range(part_slots):
+                    near_g[pair_rows(c * tile_rows + r), slot * pixels:(slot + 1) * pixels] = joined(
+                        near_block(r, c, slot), near_block(r + 1, c, slot))
+            return carry
+
+        lax.fori_loop(0, tile_cols, gather, 0)
         product = lax.dot_general(
-            near_g[sub * near_slots + slot], near_w[sub, :, where], contract, preferred_element_type=jnp.float32)
-        if first:
+            near_g[...], near_w[sub, :, base * pixels:(base + part_slots) * pixels], contract,
+            preferred_element_type=jnp.float32)
+        if part == 0:
             near_acc[...] = product
         else:
             near_acc[...] += product
 
-    near_dot(True, 0, 0)
-
-    def near_step(t, carry):
-        near_dot(False, t // near_slots, t % near_slots)
-        return carry
-
-    lax.fori_loop(1, 2 * near_slots, near_step, 0)
-
-    level_at = tile_cols * (near_slots + far_slots)
-    far_at = tile_cols * near_slots
-    chunk_blocks = tile_rows * chunk_cols
-    chunk_rows = chunk_blocks * half
-
-    def block_rows(block):
-        return pl.ds(pl.multiple_of(block * half, half), half)
+    level_at = near_slots + far_slots
 
     def far_chunk(k):
-        def gather_far(who, base):
-            def body(t, carry):
-                at = pl.ds(pl.multiple_of(base + t * 2 * half, 2 * half), 2 * half)
-                for sub in range(2):
-                    for slot in range(far_slots):
-                        parts = []
-                        for step in range(2):
-                            block = 2 * t + step
-                            r, c = block // chunk_cols, block % chunk_cols
-                            row = codes_s[who, sub, r, far_at + (k * chunk_cols + c) * far_slots + slot]
-                            parts.append(far[k][row, c].astype(jnp.float32))
-                        far_g[sub * far_slots + slot, at, :] = jnp.concatenate(parts, axis=0).astype(jnp.bfloat16)
+        rows = sizes[k] * tile_rows * half
+
+        def gather_far(who):
+            def far_block(r, c, sub, slot):
+                row = codes_s[who, sub, r, near_slots + slot, starts[k] + c]
+                return far[k][row, c]
+
+            def body(c, carry):
+                for r in range(0, tile_rows, 2):
+                    for sub in range(2):
+                        for slot in range(far_slots):
+                            at = sub * far_slots + slot
+                            far_g[pair_rows((who * sizes[k] + c) * tile_rows + r), at * pixels:(at + 1) * pixels] = joined(
+                                far_block(r, c, sub, slot), far_block(r + 1, c, sub, slot))
                 return carry
 
-            lax.fori_loop(0, chunk_blocks // 2, body, 0)
-
-        gather_far(0, 0)
+            lax.fori_loop(0, sizes[k], body, 0)
+
+        gather_far(0)
 
         @pl.when(is_helper)
         def _():
-            gather_far(1, chunk_rows)
-
-        for sub in range(2):
-            for slot in range(far_slots):
-                product = lax.dot_general(
-                    far_g[sub * far_slots + slot], far_w[sub, :, slot * pixels:(slot + 1) * pixels],
-                    contract, preferred_element_type=jnp.float32)
-                if sub + slot == 0:
-                    far_acc[...] = product
-                else:
-                    far_acc[...] += product
+            gather_far(1)
+
+        depth = far_slots * pixels
+        product = lax.dot_general(
+            far_g[:2 * rows, :depth], far_w[0], contract, preferred_element_type=jnp.float32)
+        product += lax.dot_general(
+            far_g[:2 * rows, depth:], far_w[1], contract, preferred_element_type=jnp.float32)
+        far_acc[pl.ds(starts[k] * tile_rows * half, rows), :] = product[:rows]
+        end_acc[pl.ds(0, rows), :] = product[rows:]
 
         @pl.when(is_helper)
         def _():
-            def body(block, carry):
-                r, c = block // chunk_cols, block % chunk_cols
-                value = far[k][end_tile * tile_rows + r, c].astype(jnp.float32)
-                mean = far_acc[block_rows(chunk_blocks + block), :]
-                white_src[r, k * chunk_cols + c] = (value - mean).astype(jnp.bfloat16)
+            def body(c, carry):
+                for r in range(tile_rows):
+                    value = far[k][end_tile * tile_rows + r, c].astype(jnp.float32)
+                    white_src[r, starts[k] + c] = (value - end_acc[block_rows(c * tile_rows + r), :]).astype(jnp.bfloat16)
                 return carry
 
-            lax.fori_loop(0, chunk_blocks, body, 0)
+            lax.fori_loop(0, sizes[k], body, 0)
             white_copy(k).start()
-
-        def body(block, carry):
-            r, c = block // chunk_cols, block % chunk_cols
-            col = k * chunk_cols + c
-            level = codes_s[0, 0, r, level_at + col]
-            mean = jnp.where(level == 1, near_acc[block_rows(r * tile_cols + col), :], far_acc[block_rows(block), :])
-            out[r, col] = (near[2 + r, 2 + col].astype(jnp.float32) - mean).astype(jnp.bfloat16)
-            return carry
-
-        lax.fori_loop(0, chunk_blocks, body, 0)
 
     def white_copy(k):
         return pltpu.make_async_remote_copy(
@@ -352,6 +360,7 @@
 
     @pl.when(is_mid)
     def _():
+        near_part(0)
         for k in range(chunks):
             d = n_rows - 3
             for way in (0, 1):
@@ -359,29 +368,48 @@
                 def _():
                     received(way, d, k).wait_recv()
             far_chunk(k)
+            if k < PARTS - 2:
+                near_part(k + 1)
+        near_part(PARTS - 1)
+
+        def body(c, carry):
+            for r in range(tile_rows):
+                level = codes_s[0, s, r, level_at, c]
+                at = block_rows(c * tile_rows + r)
+                mean = jnp.where(level == 1, near_acc[at, :], far_acc[at, :])
+                out[r, c] = (near[2 + r, 2 + c].astype(jnp.float32) - mean).astype(jnp.bfloat16)
+            return carry
+
+        lax.fori_loop(0, tile_cols, body, 0)
 
     @pl.when(is_end)
     def _():
+        for part in range(PARTS):
+            near_part(part)
         for k in range(chunks):
             white_copy(k).wait_recv()
 
-            def body(block, carry):
-                r, c = block // chunk_cols, block % chunk_cols
-                col = k * chunk_cols + c
-                level = codes_s[0, 0, r, level_at + col]
-                fine = near[2 + r, 2 + col].astype(jnp.float32) - near_acc[block_rows(r * tile_cols + col), :]
-                coarse = white_dst[r, col].astype(jnp.float32)
-                out[r, col] = jnp.where(level == 1, fine, coarse).astype(jnp.bfloat16)
+            def body(c, carry):
+                for r in range(tile_rows):
+                    level = codes_s[0, s, r, level_at, c]
+                    mean = near_acc[block_rows(c * tile_rows + r), :]
+                    fine = near[2 + r, 2 + c].astype(jnp.float32) - mean
+                    coarse = white_dst[r, c].astype(jnp.float32)
+                    out[r, c] = jnp.where(level == 1, fine, coarse).astype(jnp.bfloat16)
                 return carry
 
-            lax.fori_loop(0, chunk_blocks, body, 0)
+            lax.fori_loop(starts[k], starts[k + 1], body, 0)
 
     code_partner.wait_send()
 
     @pl.when(is_end)
     def _():
         code_straight.wait_send()
-        code_cross.wait_send()
+
+    for di, dx in corners:
+        @pl.when(present(di, 0) & present(0, dx))
+        def _():
+            corner_copy(di, dx).wait_send()
 
     for di, dx in offsets:
         @pl.when(side_sends(di, dx))
@@ -398,6 +426,7 @@
 
     @pl.when(is_helper)
     def _():
+        code_relay.wait_send()
         for k in range(chunks):
             white_copy(k).wait_send()
 
@@ -407,39 +436,39 @@
     n_rows, n_cols = lax.axis_size("rows"), lax.axis_size("cols")
     near_slots, far_slots = near_codes.shape[2], far_rows.shape[2]
     half = samples // 2
-    chunks = CHUNKS
-    chunk_cols = tile_cols // chunks
-    row_pos = jnp.arange(tile_rows, dtype=jnp.int32)[:, None, None]
-    col_pos = jnp.arange(tile_cols, dtype=jnp.int32)[None, :, None]
-    places = (row_pos + near_codes // 5) * (1 << ROW_STRIDE_BITS) + col_pos + near_codes % 5
+    starts = chunk_starts(tile_cols)
+    chunks = len(starts) - 1
     codes = jnp.concatenate(
-        [places.reshape(tile_rows, -1), far_rows.reshape(tile_rows, -1), block_level], axis=1)
-    width = codes.shape[1]
-    codes = jnp.pad(codes, ((0, 0), (0, -width % 128)))
-    dims = (n_rows, n_cols, tile_rows, tile_cols, half, pixels, near_slots, far_slots, chunks)
+        [jnp.transpose(near_codes, (0, 2, 1)), jnp.transpose(far_rows, (0, 2, 1)), block_level[:, None, :]], axis=1)
+    codes = jnp.pad(codes, ((0, 0), (0, -codes.shape[1] % 8), (0, -tile_cols % 128)))
+    dims = (n_rows, n_cols, tile_rows, tile_cols, half, pixels, near_slots, far_slots)
     block = (half, pixels)
     bf16, f32 = jnp.bfloat16, jnp.float32
-    chunk_rows = tile_rows * chunk_cols * half
+    all_rows = tile_rows * tile_cols * half
+    chunk_rows = tile_rows * half * max(starts[k + 1] - starts[k] for k in range(chunks))
     dma = pltpu.SemaphoreType.DMA
-    scratch = [pltpu.VMEM((n_rows * tile_rows, chunk_cols) + block, bf16) for _ in range(chunks)]
+    scratch = [pltpu.VMEM((n_rows * tile_rows, starts[k + 1] - starts[k]) + block, bf16) for k in range(chunks)]
     scratch += [
         pltpu.VMEM((tile_rows + 4, tile_cols + 4) + block, bf16),
         pltpu.VMEM((2,) + near_factor.shape, bf16),
         pltpu.VMEM((2,) + far_factor.shape, bf16),
         pltpu.VMEM((2, 2) + codes.shape, jnp.int32),
         pltpu.SMEM((2, 2) + codes.shape, jnp.int32),
-        pltpu.VMEM((2 * near_slots, tile_rows * tile_cols * half, pixels), bf16),
-        pltpu.VMEM((2 * far_slots, 2 * chunk_rows, pixels), bf16),
-        pltpu.VMEM((tile_rows * tile_cols * half, pixels), f32),
-        pltpu.VMEM((2 * chunk_rows, pixels), f32),
+        pltpu.VMEM((all_rows, 2 * near_slots // PARTS * pixels), bf16),
+        pltpu.VMEM((2 * chunk_rows, 2 * far_slots * pixels), bf16),
+        pltpu.VMEM((all_rows, pixels), f32),
+        pltpu.VMEM((all_rows, pixels), f32),
+        pltpu.VMEM((chunk_rows, pixels), f32),
         pltpu.VMEM((tile_rows, tile_cols) + block, bf16),
         pltpu.VMEM((tile_rows, tile_cols) + block, bf16),
         dma((2, n_rows - 2, chunks)),
         dma((2, n_rows - 2, chunks)),
         dma((chunks,)),
         dma((chunks,)),
-        dma((8,)),
-        dma((8,)),
+        dma((4,)),
+        dma((4,)),
+        dma((4,)),
+        dma((4,)),
         dma((3,)),
         dma((3,)),
         dma((2,)),

time: 47.4 us -> 42.5 us (0.90)
  Pallas kernels: 42.1 us -> 38.9 us
  local copies, waits for them, and re-layouts: 3.5 us -> 2.48 us
  other arithmetic: 1.48 us -> 0.74 us
    pallas_call x1, Pallas kernels: 42.1 us -> 38.9 us  [on_device(): pl.pallas_call(functools.partial(kernel, dims), out_shape=jax.ShapeDtypeS...]
    unnamed x2 -> x1, local copies, waits for them, and re-layouts: 2.65 us -> 1.87 us
    add x1 -> x0, other arithmetic: 0.72 us -> none  [on_device(): (row_pos + near_codes // 5) * (1 << ROW_STRIDE_BITS) + col_pos]
where the time goes in v2:
time: 42.5 us; the launch traced here: 42.1 us
  Pallas kernels  38.9 us (92%)
  local copies, waits for them, and re-layouts  2.48 us (6%)
  other arithmetic  0.74 us (2%)
    pallas_call x1, Pallas kernels, on_device(): pl.pallas_call(functools.partial(kernel, dims), out_shape=jax.ShapeDtypeS...  38.9 us
    unnamed x1, local copies, waits for them, and re-layouts  1.87 us

profile of v2, /device:TPU:0, one launch (start us, length us, event | category | flops | bytes accessed | tf_op | source)
XLA Modules:
  0.0 42.1 jit_solution(3917603082772983377)
XLA Ops:
  0.0 0.7 %pad_add_fusion = s32[4,7,16]{2,1,0:T(8,128)S(1)} fusion(s32[4,1,16]{2,1,0:T(1,128)} %bitcast.7, s32[4,2,16]{2,1,0:T(2,128)} %bitcast.6, s32[4,4,16]{2,1,0:T(4,128)} %bitcast.5), kind=kLoop, calls=%fused_computation | loop fusion | flops 896 | bytes 3584 | tf_op jit(solution)/shard_map/concatenate | solution.py:441
  0.7 0.6 %pad.4.codes = s32[4,8,128]{2,1,0:T(8,128)} pad(s32[4,7,16]{2,1,0:T(8,128)S(1)} %pad_add_fusion, s32[]{:T(128)} %constant.0.clone.1), padding=0_0x0_1x0_112 | pad | bytes 18180 | tf_op jit(solution)/shard_map/jit(_pad)/pad | solution.py:443
  1.4 38.9 %shard_map.64 = bf16[4,16,8,512]{3,2,1,0:T(8,128)(2,1)} custom-call(bf16[4,16,16,512]{3,2,1,0:T(8,128)(2,1)} %conv.1, s32[4,8,128]{2,1,0:T(8,128)} %pad.4.codes, bf16[512,2048]{1,0:T(8,128)(2,1)} %near_factor.1, bf16[512,1024]{1,0:T(8,128)(2,1)} %far_factor.1), custom_call_target="tpu_custom_call" | custom-call | tf_op jit(solution)/shard_map/pallas_call | solution.py:481
  40.3 1.9 %copy.9 = bf16[4,16,8,512]{3,2,1,0:T(8,128)(2,1)} copy(bf16[4,16,8,512]{3,2,1,0:T(8,128)(2,1)} %shard_map.64) | data formatting | bytes 1048576

commit v3 on v2

--- a/solution.py
+++ b/solution.py
@@ -440,7 +440,6 @@
     chunks = len(starts) - 1
     codes = jnp.concatenate(
         [jnp.transpose(near_codes, (0, 2, 1)), jnp.transpose(far_rows, (0, 2, 1)), block_level[:, None, :]], axis=1)
-    codes = jnp.pad(codes, ((0, 0), (0, -codes.shape[1] % 8), (0, -tile_cols % 128)))
     dims = (n_rows, n_cols, tile_rows, tile_cols, half, pixels, near_slots, far_slots)
     block = (half, pixels)
     bf16, f32 = jnp.bfloat16, jnp.float32

time: 42.5 us -> 42.4 us (level)
  local copies, waits for them, and re-layouts: 2.48 us -> 1.87 us
  other arithmetic: 0.74 us -> 1.34 us
    pad x1 -> x0, local copies, waits for them, and re-layouts: 0.61 us -> none  [on_device(): jnp.pad(codes, ((0, 0), (0, -codes.shape[1] % 8), (0, -tile_cols % 128)))]
    concatenate x1, other arithmetic: 0.74 us -> 1.34 us  [on_device(): jnp.concatenate([jnp.transpose(near_codes, (0, 2, 1)), jnp.transpose(far_...]
where the time goes in v3:
time: 42.4 us; the launch traced here: 42.1 us
  Pallas kernels  38.9 us (92%)
  local copies, waits for them, and re-layouts  1.87 us (4%)
  other arithmetic  1.34 us (3%)
    pallas_call x1, Pallas kernels, on_device(): pl.pallas_call(functools.partial(kernel, dims), out_shape=jax.ShapeDtypeS...  38.9 us
    unnamed x1, local copies, waits for them, and re-layouts  1.87 us
    concatenate x1, other arithmetic, on_device(): jnp.concatenate([jnp.transpose(near_codes, (0, 2, 1)), jnp.transpose(far_...  1.34 us

profile of v3, /device:TPU:0, one launch (start us, length us, event | category | flops | bytes accessed | tf_op | source)
XLA Modules:
  0.0 42.1 jit_solution(16879331448474158465)
XLA Ops:
  0.0 1.3 %pad_add_fusion.codes = s32[4,7,16]{2,1,0:T(8,128)} fusion(s32[4,1,16]{2,1,0:T(1,128)} %bitcast.7, s32[4,2,16]{2,1,0:T(2,128)} %bitcast.6, s32[4,4,16]{2,1,0:T(4,128)} %bitcast.5), kind=kLoop, calls=%fused_computation | loop fusion | flops 896 | bytes 3584 | tf_op jit(solution)/shard_map/concatenate | solution.py:441
  1.3 38.9 %shard_map.64 = bf16[4,16,8,512]{3,2,1,0:T(8,128)(2,1)} custom-call(bf16[4,16,16,512]{3,2,1,0:T(8,128)(2,1)} %conv.1, s32[4,7,16]{2,1,0:T(8,128)} %pad_add_fusion.codes, bf16[512,2048]{1,0:T(8,128)(2,1)} %near_factor.1, bf16[512,1024]{1,0:T(8,128)(2,1)} %far_factor.1), custom_call_target="tpu_custom_call" | custom-call | tf_op jit(solution)/shard_map/pallas_call | solution.py:480
  40.3 1.9 %copy.9 = bf16[4,16,8,512]{3,2,1,0:T(8,128)(2,1)} copy(bf16[4,16,8,512]{3,2,1,0:T(8,128)(2,1)} %shard_map.64) | data formatting | bytes 1048576
